TPU v7x, 256 devices: a whole 4x4x8 slice. The times are simulated.
256 devices in a mesh: expert: 8 (over x_hi, y), dp: 32 (over x_lo, z, core).
Axes of the slice: x: 4 (x_hi: 2, x_lo: 2; x = x_hi * 2 + x_lo), y: 4, z: 8, core: 2. Of those that a mesh axis runs over, the one named last changes fastest.
Arguments:
- tokens: bfloat16 [2048, 4096], P(('expert', 'dp')), may hold values from -6 to 6
- routes: int32 [2048, 2], P(('expert', 'dp')), may hold values from 0 to 7, all different within a row; in each aligned block of 8 rows (0 to 7, 8 to 15, ...) at most 3 rows name the same one
- route_weights: float32 [2048, 2], P(('expert', 'dp')), may hold values from 0.2 to 1
- w_gate: bfloat16 [8, 4096, 14336], P('expert', None, 'dp'), may hold values from -0.09375 to 0.09375
- w_up: bfloat16 [8, 4096, 14336], P('expert', None, 'dp'), may hold values from -0.09375 to 0.09375
- w_down: bfloat16 [8, 14336, 4096], P('expert', 'dp'), may hold values from -0.046875 to 0.046875
Outputs:
- mixed: bfloat16 [2048, 4096], P(('expert', 'dp'))
Inputs may be any that keep to these rules, and one draw needn't show every extreme that they name: `routes`: within the rows of one device (aligned blocks of 8 rows) the two experts of a token differ and no expert is named more than 3 times; in every draw some block names some expert exactly 3 times. Every expert is named somewhere.
All inputs are finite; a program needn't handle non-finite values.
Results may differ from a plain program's by a relative error of at most 0.0057.
Values may be sent and summed in bfloat16 or wider, within the bound.
No kernel may reach another device: no remote copies, remote signals or barrier semaphores. Data moves between devices by JAX's collectives and lax.ppermute only.
A program may use at most 128 MiB of HBM per device.

v0:
```python
import jax
import jax.numpy as jnp
from jax import lax
from jax.sharding import PartitionSpec as P


def expert_projection(gate_local, up_local, down_local):

    def project(block_rows, first_row):
        gated = jnp.dot(block_rows, gate_local, preferred_element_type=jnp.float32)
        upward = jnp.dot(block_rows, up_local, preferred_element_type=jnp.float32)
        hidden = (jax.nn.silu(gated) * upward).astype(jnp.bfloat16)
        return jnp.dot(hidden, down_local, preferred_element_type=jnp.float32)

    return project


def local(tokens, routes, route_weights, w_gate, w_up, w_down):
    groups = lax.axis_size("expert")
    tok_count = tokens.shape[0]
    features = tokens.shape[1]
    capacity = 3 * tok_count // groups
    columns = groups * capacity
    listed = routes.reshape(2 * tok_count)
    chosen = (listed[:, None] == jnp.arange(groups, dtype=jnp.int32)[None, :]).astype(jnp.int32)
    before = jnp.cumsum(chosen, axis=0) - chosen
    column = listed * capacity + jnp.sum(before * chosen, axis=1)
    placing = (column[:, None] == jnp.arange(columns, dtype=jnp.int32)[None, :]).astype(
        jnp.bfloat16
    )
    placing = placing.reshape(tok_count, 2, columns)
    sending = jnp.sum(placing, axis=1)
    outgoing = jnp.einsum("tw,td->wd", sending, tokens, preferred_element_type=jnp.float32).astype(
        jnp.bfloat16
    )
    arrived = lax.all_to_all(
        outgoing.reshape(groups, capacity, features),
        "expert",
        split_axis=0,
        concat_axis=0,
        tiled=True,
    )
    arrived = arrived.reshape(columns, features)
    project = expert_projection(w_gate[0], w_up[0], w_down[0])
    partials = project(lax.all_gather(arrived, "dp", axis=0, tiled=True), jnp.int32(0))
    summed = lax.psum_scatter(partials, "dp", scatter_dimension=0, tiled=True)
    results = summed.astype(jnp.bfloat16).reshape(groups, capacity, features)
    returned = lax.all_to_all(results, "expert", split_axis=0, concat_axis=0, tiled=True).reshape(
        columns, features
    )
    picked = jnp.einsum("tkw,wd->tkd", placing, returned, preferred_element_type=jnp.float32)
    combined = jnp.sum(route_weights[:, :, None] * picked, axis=1)
    return combined.astype(jnp.bfloat16)


def solution(mesh):
    placed = (
        P(("expert", "dp"), None),
        P(("expert", "dp"), None),
        P(("expert", "dp"), None),
        P("expert", None, "dp"),
        P("expert", None, "dp"),
        P("expert", "dp", None),
    )
    return jax.shard_map(
        local, mesh=mesh, in_specs=placed, out_specs=P(("expert", "dp"), None), check_vma=False
    )
```

profile of v0, /device:TPU:8, one launch (start us, length us, event | category | flops | bytes accessed | tf_op | source)
XLA Modules:
  0.0 278.0 jit_solution(10584551748539052171)
XLA Ops:
  6.5 0.0 copy-start
  6.5 0.0 all-gather.2.cloned.1.call-start
  6.5 0.8 copy.13
  7.3 0.1 eq.51
  7.4 0.1 fusion.16
  7.5 0.2 select_reduce_fusion
  7.7 0.1 reduce_sum.33
  7.8 0.1 copy.15
  7.9 0.1 fusion.20
  8.0 0.0 copy-done
  8.0 0.3 convolution_convert_fusion
  8.2 0.1 reshape.54
  8.4 14.1 %all_to_all.10 = bf16[8,3,4096]{2,1,0:T(4,128)(2,1)S(1)} all-to-all(bf16[8,3,4096]{2,1,0:T(4,128)(2,1)S(1)} %reshape.54), channel_id=1, replica_groups=mesh['expert'=8,'dp'=32] {'expert'}, dimensions={0} | all-to-all | bytes 393216 | tf_op jit(solution)/shard_map/all_to_all | solution.py:36
  22.5 0.8 reshape.55
  23.3 0.0 all-gather.2.cloned.1.call-update
  23.3 0.0 reduce-scatter.2.cloned.1.call-start
  23.4 69.3 %all-gather.2.cloned.1.call-done = bf16[768,4096]{1,0:T(8,128)(2,1)} async-done(((bf16[24,4096]{1,0:T(8,128)(2,1)}), bf16[768,4096]{1,0:T(8,128)(2,1)}) %all-gather.2.cloned.1.call-update) | async-done | bytes 6291472 | tf_op jit(solution)/shard_map/all_gather | solution.py:45
  92.6 6.9 %fusion.4 = f32[768,448]{0,1:T(8,128)S(1)} fusion(bf16[768,4096]{1,0:T(8,128)(2,1)} %all-gather.2.cloned.1.call-done, bf16[1,4096,448]{1,2,0:T(8,128)(2,1)} %param.9), kind=kOutput, calls=%fused_computation.6 | convolution fusion | flops 2818572288 | bytes 11337728 | tf_op jit(solution)/shard_map/dot_general | solution.py:10
  99.5 17.9 %fusion = f32[768,4096]{1,0:T(8,128)} fusion(bf16[1,448,4096]{2,1,0:T(8,128)(2,1)} %param.11, bf16[768,4096]{1,0:T(8,128)(2,1)} %all-gather.2.cloned.1.call-done, bf16[1,4096,448]{1,2,0:T(8,128)(2,1)} %param.10, f32[768,448]{0,1:T(8,128)S(1)} %fusion.4), kind=kOutput, calls=%fused_computation.2 | convolution fusion | flops 5639208960 | bytes 27590656 | tf_op jit(solution)/shard_map/dot_general | solution.py:13
  117.4 0.0 copy-start.1
  117.4 0.0 reduce-scatter.2.cloned.1.call-update
  117.4 137.9 %reduce-scatter.2.cloned.1.call-done = f32[24,4096]{1,0:T(8,128)} async-done(((f32[768,4096]{1,0:T(8,128)}), f32[24,4096]{1,0:T(8,128)}) %reduce-scatter.2.cloned.1.call-update) | async-done | bytes 393232 | tf_op jit(solution)/shard_map/reduce_scatter | solution.py:46
  255.4 1.0 convert_element_type.25
  256.4 0.1 reshape.56
  256.5 13.6 %all_to_all.11 = bf16[8,3,4096]{2,1,0:T(4,128)(2,1)S(1)} all-to-all(bf16[8,3,4096]{2,1,0:T(4,128)(2,1)S(1)} %reshape.56), channel_id=1, replica_groups=mesh['expert'=8,'dp'=32] {'expert'}, dimensions={0} | all-to-all | bytes 393216 | tf_op jit(solution)/shard_map/all_to_all | solution.py:48
  270.2 0.2 reshape.58
  270.3 0.0 copy-done.1
  270.3 0.9 fusion.12
  (2 shorter events, 0.0 us)
Async XLA Ops:
  6.5 1.4 copy-start
  6.5 86.1 %all-gather.2.cloned.1.call-start = ((), (), s32[]{:S(2)}) async-start(), calls=%async_computation.3 | async-start | bytes 6488064 | tf_op jit(solution)/shard_map/all_gather | solution.py:45
  23.3 232.0 %reduce-scatter.2.cloned.1.call-start = ((), (), s32[]{:S(2)}) async-start(), calls=%async_computation.4 | async-start | bytes 12976128 | tf_op jit(solution)/shard_map/reduce_scatter | solution.py:46
  117.4 152.9 %copy-start.1 = (f32[8,2]{0,1:T(2,128)S(1)}, f32[8,2]{0,1:T(2,128)}, u32[]{:S(2)}) copy-start(f32[8,2]{0,1:T(2,128)} %param.8) | copy-start | bytes 196
Sparse Core Ops, SparseCore 0:
  23.4 69.1 all-gather.1
  117.6 137.7 reduce-scatter.1
where the time goes:
time: 278 us
  waiting for transfers between devices  207 us (74%)
  blocking collectives  27.7 us (10%)
  matrix products  25.9 us (9%)
  between operations  13.5 us (5%)
    reduce_scatter x1, waiting for transfers between devices, local(): summed = lax.psum_scatter(partials, 'dp', scatter_dimension=0, tiled=True)  138 us
    all_gather x1, waiting for transfers between devices, local(): lax.all_gather(arrived, 'dp', axis=0, tiled=True)  69.3 us
    dot_general x1, matrix products, project(): return jnp.dot(hidden, down_local, preferred_element_type=jnp.float32)  17.9 us
    all_to_all x1, blocking collectives, local(): lax.all_to_all(outgoing.reshape(groups, capacity, features), 'expert', sp...  14.1 us
    all_to_all x1, blocking collectives, local(): lax.all_to_all(results, 'expert', split_axis=0, concat_axis=0, tiled=True)  13.6 us
    dot_general x1, matrix products, project(): gated = jnp.dot(block_rows, gate_local, preferred_element_type=jnp.float32)  6.9 us
  transfers between devices with their start and end apart: 2, of which 2 were waited for; matrix products, arithmetic and copies ran while one was open for 0% of the time, Pallas kernels for 0%

commit v1 on v0

--- a/solution.py
+++ b/solution.py
@@ -2,6 +2,10 @@
 import jax.numpy as jnp
 from jax import lax
 from jax.sharding import PartitionSpec as P
+
+choose_ranges_in = lambda v0, ax_name: jnp.concatenate(
+    lax.all_to_all(jnp.stack([v0] * lax.axis_size(ax_name)), ax_name, 0, 0), axis=0
+)
 
 
 def expert_projection(gate_local, up_local, down_local):
@@ -42,7 +46,7 @@
     )
     arrived = arrived.reshape(columns, features)
     project = expert_projection(w_gate[0], w_up[0], w_down[0])
-    partials = project(lax.all_gather(arrived, "dp", axis=0, tiled=True), jnp.int32(0))
+    partials = project(choose_ranges_in(arrived, "dp"), jnp.int32(0))
     summed = lax.psum_scatter(partials, "dp", scatter_dimension=0, tiled=True)
     results = summed.astype(jnp.bfloat16).reshape(groups, capacity, features)
     returned = lax.all_to_all(results, "expert", split_axis=0, concat_axis=0, tiled=True).reshape(

time: 278 us -> 353 us (1.27)
  blocking collectives: 27.7 us -> 178 us
  waiting for transfers between devices: 207 us -> 133 us
  matrix products: 25.9 us -> 22 us
    all_to_all x0 -> x1, blocking collectives: none -> 150 us  [lax.all_to_all(jnp.stack([v0] * lax.axis_size(ax_name)), ax_name, 0, 0)]
    all_gather x1 -> x0, waiting for transfers between devices: 69.3 us -> none  [local(): lax.all_gather(arrived, 'dp', axis=0, tiled=True)]
    reduce_scatter x1, waiting for transfers between devices: 138 us -> 133 us  [local(): summed = lax.psum_scatter(partials, 'dp', scatter_dimension=0, tiled=True)]
    dot_general x1, matrix products: 6.9 us -> 3.06 us  [project(): gated = jnp.dot(block_rows, gate_local, preferred_element_type=jnp.float32)]
  transfers between devices with their start and end apart: 2 -> 1, of which waited for: 2 -> 1; matrix products, arithmetic and copies ran while one was open for 0% -> 0% of each run, Pallas kernels for 0% -> 0%
where the time goes in v1:
time: 353 us
  blocking collectives  178 us (50%)
  waiting for transfers between devices  133 us (38%)
  matrix products  22 us (6%)
  between operations  13.5 us (4%)
  local copies, waits for them, and re-layouts  5.01 us (1%)
    all_to_all x1, blocking collectives, lax.all_to_all(jnp.stack([v0] * lax.axis_size(ax_name)), ax_name, 0, 0)  150 us
    reduce_scatter x1, waiting for transfers between devices, local(): summed = lax.psum_scatter(partials, 'dp', scatter_dimension=0, tiled=True)  133 us
    dot_general x1, matrix products, project(): return jnp.dot(hidden, down_local, preferred_element_type=jnp.float32)  17.9 us
    all_to_all x1, blocking collectives, local(): lax.all_to_all(outgoing.reshape(groups, capacity, features), 'expert', sp...  14.1 us
    all_to_all x1, blocking collectives, local(): lax.all_to_all(results, 'expert', split_axis=0, concat_axis=0, tiled=True)  13.7 us
  transfers between devices with their start and end apart: 1, of which 1 were waited for; matrix products, arithmetic and copies ran while one was open for 0% of the time, Pallas kernels for 0%

profile of v1, /device:TPU:8, one launch (start us, length us, event | category | flops | bytes accessed | tf_op | source)
XLA Modules:
  0.0 352.9 jit_solution(3810686533255854404)
XLA Ops:
  6.5 0.0 copy-start
  6.5 0.0 reduce-scatter.2.cloned.1.call-start
  6.5 0.8 copy.13
  7.3 0.1 eq.51
  7.4 0.1 fusion.16
  7.5 0.2 select_reduce_fusion
  7.7 0.1 reduce_sum.33
  7.8 0.1 copy.15
  7.9 0.1 fusion.20
  8.0 0.0 copy-done
  8.0 0.3 convolution_convert_fusion
  8.2 0.1 reshape.56
  8.4 14.1 %all_to_all.15 = bf16[8,3,4096]{2,1,0:T(4,128)(2,1)S(1)} all-to-all(bf16[8,3,4096]{2,1,0:T(4,128)(2,1)S(1)} %reshape.56), channel_id=1, replica_groups=mesh['expert'=8,'dp'=32] {'expert'}, dimensions={0} | all-to-all | bytes 393216 | tf_op jit(solution)/shard_map/all_to_all | solution.py:40
  22.5 0.2 stack_reshape.2
  22.6 0.8 stack.3
  23.4 0.0 copy-start.3
  23.4 149.8 %all_to_all.16 = bf16[32,24,4096]{2,1,0:T(8,128)(2,1)S(1)} all-to-all(bf16[32,24,4096]{2,1,0:T(8,128)(2,1)S(1)} %stack.3), channel_id=1, replica_groups=mesh['expert'=8,'dp'=32] {'dp'}, dimensions={0} | all-to-all | bytes 12582912 | tf_op jit(solution)/shard_map/all_to_all | solution.py:7
  173.2 0.0 copy-start.1
  173.2 2.6 copy-done.1
  175.8 0.0 copy-done.3
  175.8 3.1 fusion.4
  178.9 17.9 %fusion = f32[768,4096]{1,0:T(8,128)} fusion(bf16[1,448,4096]{2,1,0:T(8,128)(2,1)} %param.11, bf16[768,4096]{1,0:T(8,128)(2,1)} %bitcast.25, bf16[1,4096,448]{1,2,0:T(8,128)(2,1)} %param.10, f32[768,448]{0,1:T(8,128)S(1)} %fusion.4), kind=kOutput, calls=%fused_computation.2 | convolution fusion | flops 5639208960 | bytes 27590656 | tf_op jit(solution)/shard_map/dot_general | solution.py:17
  196.7 0.0 copy-start.2
  196.7 0.0 reduce-scatter.2.cloned.1.call-update
  196.8 133.4 %reduce-scatter.2.cloned.1.call-done = f32[24,4096]{1,0:T(8,128)} async-done(((f32[768,4096]{1,0:T(8,128)}), f32[24,4096]{1,0:T(8,128)}) %reduce-scatter.2.cloned.1.call-update) | async-done | bytes 393232 | tf_op jit(solution)/shard_map/reduce_scatter | solution.py:50
  330.2 1.0 convert_element_type.25
  331.2 0.1 reshape.58
  331.3 13.7 %all_to_all.17 = bf16[8,3,4096]{2,1,0:T(4,128)(2,1)S(1)} all-to-all(bf16[8,3,4096]{2,1,0:T(4,128)(2,1)S(1)} %reshape.58), channel_id=1, replica_groups=mesh['expert'=8,'dp'=32] {'expert'}, dimensions={0} | all-to-all | bytes 393216 | tf_op jit(solution)/shard_map/all_to_all | solution.py:52
  345.0 0.2 reshape.60
  345.2 0.0 copy-done.2
  345.2 0.9 fusion.12
  (2 shorter events, 0.0 us)
Async XLA Ops:
  6.5 1.4 copy-start
  6.5 323.6 %reduce-scatter.2.cloned.1.call-start = ((), (), s32[]{:S(2)}) async-start(), calls=%async_computation.4 | async-start | bytes 12976128 | tf_op jit(solution)/shard_map/reduce_scatter | solution.py:50
  23.4 152.4 %copy-start.3 = (bf16[1,4096,448]{1,2,0:T(8,128)(2,1)S(1)}, bf16[1,4096,448]{1,2,0:T(8,128)(2,1)}, u32[]{:S(2)}) copy-start(bf16[1,4096,448]{1,2,0:T(8,128)(2,1)} %param.9) | copy-start | bytes 11010052
  173.2 2.6 copy-start.1
  196.7 148.5 %copy-start.2 = (f32[8,2]{0,1:T(2,128)S(1)}, f32[8,2]{0,1:T(2,128)}, u32[]{:S(2)}) copy-start(f32[8,2]{0,1:T(2,128)} %param.8) | copy-start | bytes 196
Sparse Core Ops, SparseCore 0:
  196.9 133.2 reduce-scatter.1
